TPU v7x, 32 devices: a whole 2x2x4 slice. The times are simulated.
32 devices in a mesh: groups: 2 (over y), lon: 4 (over z), lat: 2 (over x), dp: 2 (over core).
Axes of the slice: x: 2, y: 2, z: 4, core: 2. Of those that a mesh axis runs over, the one named last changes fastest.
Arguments:
- fields: bfloat16 [4, 32, 64, 192], P(('groups', 'dp'), 'lat', 'lon'), parts along dimension 0, may hold values from -6 to 6
- cotangent: bfloat16 [4, 32, 64, 192], P(('groups', 'dp'), 'lat', 'lon'), parts along dimension 0, may hold values from -6 to 6
- ocean_mask: int32 [32, 64], P('lat', 'lon'), may hold values from 0 to 1, as said below
- dw_kernel: float32 [7, 7, 192], replicated, may hold values from -0.875 to 0.875
- dw_bias: float32 [192], replicated, may hold values from -4 to 4
- ln_gain: float32 [192], replicated, may hold values from 0.1 to 1.9
- ln_bias: float32 [192], replicated, may hold values from -3 to 3
- w_in: bfloat16 [192, 768], replicated, may hold values from -0.4375 to 0.4375
- b_in: float32 [768], replicated, may hold values from -3 to 3
- w_out: bfloat16 [768, 192], replicated, may hold values from -0.21875 to 0.21875
- b_out: float32 [192], replicated, may hold values from -3 to 3
- layer_scale: float32 [192], replicated, may hold values from 0.3 to 1.5
Outputs:
- block_out: bfloat16 [4, 32, 64, 192], P(('groups', 'dp'), 'lat', 'lon'), parts along dimension 0
- field_grad: bfloat16 [4, 32, 64, 192], P(('groups', 'dp'), 'lat', 'lon'), parts along dimension 0
- grad_kernel: float32 [14, 7, 192], P('groups'), parts along dimension 0
- grad_dw_bias: float32 [384], P('groups'), parts along dimension 0
- grad_ln_gain: float32 [384], P('groups'), parts along dimension 0
- grad_ln_bias: float32 [384], P('groups'), parts along dimension 0
- grad_w_in: float32 [384, 768], P('groups'), parts along dimension 0
- grad_b_in: float32 [1536], P('groups'), parts along dimension 0
- grad_w_out: float32 [1536, 192], P('groups'), parts along dimension 0
- grad_b_out: float32 [384], P('groups'), parts along dimension 0
- grad_scale: float32 [384], P('groups'), parts along dimension 0
There are 2 independent parts, one for each index of `groups`. A program takes and returns all parts, laid end to end along the dimension named above; an argument that names none is the same for every part. Nothing has to cross between parts.
Inputs may be any that keep to these rules, and one draw needn't show every extreme that they name: `ocean_mask`: each device's tile of 16 x 16 cells holds at most 192 ocean cells, and some tile holds exactly 192.
All inputs are finite; a program needn't handle non-finite values.
Results may differ from a plain program's by a relative error of at most 0.0065.
Values may be sent and summed in bfloat16 or wider, within the bound.
No kernel may reach another device: no remote copies, remote signals or barrier semaphores. Data moves between devices by JAX's collectives and lax.ppermute only.
A program may use at most 64 MiB of HBM per device.

v0:
```python
import math
import jax
import jax.numpy as jnp
from jax import lax
from jax.sharding import PartitionSpec as P

EPS = 1e-06


def padded_2(block, sides, width, periodic):
    for axis, dim in sides:
        count = lax.axis_size(axis)
        forward = [(i, i + 1) for i in range(count - 1)]
        if periodic:
            forward.append((count - 1, 0))
        backward = [(target, source) for source, target in forward]
        low = lax.ppermute(
            lax.slice_in_dim(block, block.shape[dim] - width, None, axis=dim), axis, forward
        )
        high = lax.ppermute(lax.slice_in_dim(block, 0, width, axis=dim), axis, backward)
        block = jnp.concatenate([low, block, high], axis=dim)
    return block


def depthwise(padded, kernel, tile_h, tile_w):
    total = jnp.zeros(padded.shape[:-3] + (tile_h, tile_w, padded.shape[-1]), jnp.float32)
    for row_off in range(7):
        for col_off in range(7):
            total = (
                total
                + padded[..., row_off : row_off + tile_h, col_off : col_off + tile_w, :]
                * kernel[row_off, col_off]
            )
    return total


def depthwise_back(padded, kernel, tile_h, tile_w):
    total = jnp.zeros(padded.shape[:-3] + (tile_h, tile_w, padded.shape[-1]), jnp.float32)
    for row_off in range(7):
        for col_off in range(7):
            total = (
                total
                + padded[
                    ..., 6 - row_off : 6 - row_off + tile_h, 6 - col_off : 6 - col_off + tile_w, :
                ]
                * kernel[row_off, col_off]
            )
    return total


def kernel_grad(grad, padded, tile_h, tile_w):
    lead = tuple(range(grad.ndim - 1))
    return jnp.stack(
        [
            jnp.stack(
                [
                    jnp.sum(
                        grad
                        * padded[..., row_off : row_off + tile_h, col_off : col_off + tile_w, :],
                        axis=lead,
                    )
                    for col_off in range(7)
                ]
            )
            for row_off in range(7)
        ]
    )


def gelu_tanh(values):
    return jax.nn.gelu(values, approximate=True)


def mlp_pass(act_rows, out_grad, w_in, b_in, w_out, b_out, layer_scale):
    pre = jnp.dot(act_rows, w_in, preferred_element_type=jnp.float32) + b_in
    hidden, gelu_back = jax.vjp(gelu_tanh, pre)
    hidden_b = hidden.astype(jnp.bfloat16)
    branch = jnp.dot(hidden_b, w_out, preferred_element_type=jnp.float32) + b_out
    branch_grad = out_grad * layer_scale
    branch_b = branch_grad.astype(jnp.bfloat16)
    hidden_grad = jnp.dot(branch_b, w_out.T, preferred_element_type=jnp.float32)
    pre_grad = gelu_back(hidden_grad)[0]
    pre_b = pre_grad.astype(jnp.bfloat16)
    act_grad = jnp.dot(pre_b, w_in.T, preferred_element_type=jnp.float32)
    grads = (
        jnp.dot(act_rows.T, pre_b, preferred_element_type=jnp.float32),
        jnp.sum(pre_grad, axis=0),
        jnp.dot(hidden_b.T, branch_b, preferred_element_type=jnp.float32),
        jnp.sum(branch_grad, axis=0),
        jnp.sum(out_grad * branch, axis=0),
    )
    return (branch, act_grad, grads)


def body(
    fields,
    cotangent,
    ocean_mask,
    dw_kernel,
    dw_bias,
    ln_gain,
    ln_bias,
    w_in,
    b_in,
    w_out,
    b_out,
    layer_scale,
):
    snapshots, tile_h, tile_w, channels = fields.shape
    cells = tile_h * tile_w
    ocean = ocean_mask.astype(jnp.float32)[None, :, :, None]
    start_b = fields * ocean_mask.astype(jnp.bfloat16)[None, :, :, None]
    lat_ext = padded_2(start_b, (("lat", 1),), 3, False)
    padded = padded_2(lat_ext, (("lon", 2),), 3, True).astype(jnp.float32)
    start = start_b.astype(jnp.float32)
    conv_out = depthwise(padded, dw_kernel, tile_h, tile_w) + dw_bias
    center = jnp.mean(conv_out, axis=-1, keepdims=True)
    shifted = conv_out - center
    inv_std = lax.rsqrt(jnp.mean(shifted * shifted, axis=-1, keepdims=True) + EPS)
    normed = shifted * inv_std
    act = (normed * ln_gain + ln_bias).astype(jnp.bfloat16)
    out_grad = cotangent.astype(jnp.float32) * ocean
    flat_branch, flat_act_grad, mlp_sums = mlp_pass(
        act.reshape(-1, channels),
        out_grad.reshape(-1, channels),
        w_in,
        b_in,
        w_out,
        b_out,
        layer_scale,
    )
    branch = flat_branch.reshape(fields.shape)
    act_grad = flat_act_grad.reshape(fields.shape)
    block_out = (ocean * (start + layer_scale * branch)).astype(jnp.bfloat16)
    scaled = act_grad * ln_gain
    conv_grad = inv_std * (
        scaled
        - jnp.mean(scaled, axis=-1, keepdims=True)
        - normed * jnp.mean(scaled * normed, axis=-1, keepdims=True)
    )
    grad_lat = padded_2(conv_grad.astype(jnp.bfloat16), (("lat", 1),), 3, False).astype(
        conv_grad.dtype
    )
    grad_padded = padded_2(grad_lat.astype(jnp.bfloat16), (("lon", 2),), 3, True).astype(
        grad_lat.dtype
    )
    field_grad = (
        ocean * (out_grad + depthwise_back(grad_padded, dw_kernel, tile_h, tile_w))
    ).astype(jnp.bfloat16)
    lead = (0, 1, 2)
    local = (
        kernel_grad(conv_grad, padded, tile_h, tile_w),
        jnp.sum(conv_grad, axis=lead),
        jnp.sum(act_grad * normed, axis=lead),
        jnp.sum(act_grad, axis=lead),
    ) + mlp_sums
    members = lax.axis_size("lon") * lax.axis_size("lat") * lax.axis_size("dp")
    factor = 1.0 / math.sqrt(snapshots * cells * members)
    summed = lax.psum(
        (local[0], local[1], local[2], local[3], local[4], local[5], local[6], local[7], local[8]),
        ("lon", "lat", "dp"),
    )
    finals = [piece * factor for piece in summed]
    return (
        block_out,
        field_grad,
        finals[0],
        finals[1],
        finals[2],
        finals[3],
        finals[4],
        finals[5],
        finals[6],
        finals[7],
        finals[8],
    )


def solution(mesh):
    return jax.shard_map(
        body,
        mesh=mesh,
        in_specs=(
            P(("groups", "dp"), "lat", "lon", None),
            P(("groups", "dp"), "lat", "lon", None),
            P("lat", "lon"),
            P(),
            P(),
            P(),
            P(),
            P(),
            P(),
            P(),
            P(),
            P(),
        ),
        out_specs=(
            P(("groups", "dp"), "lat", "lon", None),
            P(("groups", "dp"), "lat", "lon", None),
            P("groups", None, None),
            P("groups"),
            P("groups"),
            P("groups"),
            P("groups", None),
            P("groups"),
            P("groups", None),
            P("groups"),
            P("groups"),
        ),
        check_vma=False,
    )
```

profile of v0, /device:TPU:0, one launch (start us, length us, event | category | flops | bytes accessed | tf_op | source)
XLA Modules:
  0.0 214.5 jit_solution(16185889891956108017)
XLA Ops:
  7.2 0.8 fusion.69
  8.0 1.0 broadcast_multiply_fusion.2
  9.0 4.9 %collective-permute-start = (bf16[1,3,16,192]{3,2,1,0:T(8,128)(2,1)S(1)}, bf16[1,3,16,192]{3,2,1,0:T(8,128)(2,1)S(1)}, u32[]{:S(2)}, u32[]{:S(2)}) collective-permute-start(bf16[1,3,16,192]{3,2,1,0:T(8,128)(2,1)S(1)} %get-tuple-element.86), channel_id=1, source_target_pairs={{0,2},{1,3},{4,6},{5,7},{8,10},{9,11},{12,14},{13,15},{16,18},{17,... | collective-permute-start | bytes 55304 | tf_op jit(solution)/shard_map/ppermute | solution.py:17
  13.9 1.3 collective-permute-start.1
  15.6 4.1 %collective-permute-done.1 = bf16[1,3,16,192]{3,2,1,0:T(8,128)(2,1)S(1)} collective-permute-done((bf16[1,3,16,192]{3,2,1,0:T(8,128)(2,1)S(1)}, bf16[1,3,16,192]{3,2,1,0:T(8,128)(2,1)S(1)}, u32[]{:S(2)}, u32[]{:S(2)}) %collective-permute-start.1) | collective-permute-done | bytes 18464 | tf_op jit(solution)/shard_map/ppermute | solution.py:20
  19.7 1.6 collective-permute-start.2
  21.3 2.2 %collective-permute-start.3 = (bf16[1,22,3,192]{3,2,1,0:T(4,128)(2,1)S(1)}, bf16[1,22,3,192]{3,2,1,0:T(4,128)(2,1)S(1)}, u32[]{:S(2)}, u32[]{:S(2)}) collective-permute-start(bf16[1,22,3,192]{3,2,1,0:T(4,128)(2,1)S(1)} %get-tuple-element.81), channel_id=1, source_target_pairs={{4,0},{8,4},{12,8},{0,12},{5,1},{9,5},{13,9},{1,13},{6,2},{10,6},{... | collective-permute-start | bytes 76040 | tf_op jit(solution)/shard_map/ppermute | solution.py:20
  23.6 0.6 fusion.68
  24.2 1.5 collective-permute-done.2
  26.7 2.4 %fusion.63 = (f32[16,16]{1,0:T(8,128)S(1)}, f32[1,16,16,192]{3,2,1,0:T(8,128)S(1)}) fusion(f32[192]{0:T(256)S(1)} %copy-done.90, f32[192]{0:T(256)S(1)} %bitcast.228, f32[1,22,22,192]{3,2,1,0:T(8,128)S(1)} %maximum_convert_fusion, f32[192]{0:T(256)} %bitcast.47, f32[192]{0:T(256)S(1)} %bitcast.136, f32[192]{0:T(256)S(1)} %bitcast.138, f32[192]{0:T(256)S(1)} %bitcast.140, ...), kind=kLoop, calls=%fused_computation.208 | loop fusion | flops 4865792 | bytes 9869824 | tf_op jit(solution)/shard_map/reduce_sum | solution.py:117
  29.5 0.6 copy-done.1
  31.3 0.7 copy-done.3
  32.1 1.4 multiply_reduce_fusion
  33.5 1.3 fusion.70
  34.8 1.0 fusion.62
  36.2 0.7 multiply_reduce_fusion.2
  38.6 1.2 fusion.61
  39.8 1.1 fusion.57
  42.0 58.4 %all-reduce = (f32[7,7,192]{2,1,0:T(8,128)S(1)}, f32[192]{0:T(256)S(1)}, f32[192]{0:T(256)S(1)}, f32[192]{0:T(256)S(1)}, f32[768]{0:T(1024)S(1)}, /*index=5*/f32[192]{0:T(256)S(1)}, f32[192]{0:T(256)S(1)}) all-reduce(f32[7,7,192]{2,1,0:T(8,128)S(1)} %constant_dynamic-update-s, ...), channel_id=1, replica_groups=mesh['groups'=2,'lon'=4,'lat'=2,'dp'=2] {'lon','lat','dp'}, use_global_device_ids=true, to_apply=%region_53.0 | all-reduce | flops 11136 | bytes 89088 | tf_op jit(solution)/shard_map/psum | solution.py:159
  100.4 0.6 broadcast_multiply_fusion.3
  101.0 0.6 broadcast_multiply_fusion.6
  101.6 1.3 collective-permute-start.4
  102.9 1.3 collective-permute-start.5
  104.2 0.6 broadcast_multiply_fusion.7
  104.8 0.6 broadcast_multiply_fusion.9
  105.3 3.3 %collective-permute-done.5 = bf16[1,3,16,192]{3,2,1,0:T(8,128)(2,1)S(1)} collective-permute-done((bf16[1,3,16,192]{3,2,1,0:T(8,128)(2,1)S(1)}, bf16[1,3,16,192]{3,2,1,0:T(8,128)(2,1)S(1)}, u32[]{:S(2)}, u32[]{:S(2)}) %collective-permute-start.5) | collective-permute-done | bytes 18464 | tf_op jit(solution)/shard_map/ppermute | solution.py:20
  108.7 3.8 %collective-permute-start.7 = (bf16[1,22,3,192]{3,2,1,0:T(4,128)(2,1)S(1)}, bf16[1,22,3,192]{3,2,1,0:T(4,128)(2,1)S(1)}, u32[]{:S(2)}, u32[]{:S(2)}) collective-permute-start(bf16[1,22,3,192]{3,2,1,0:T(4,128)(2,1)S(1)} %get-tuple-element.79), channel_id=1, source_target_pairs={{4,0},{8,4},{12,8},{0,12},{5,1},{9,5},{13,9},{1,13},{6,2},{10,6},{... | collective-permute-start | bytes 76040 | tf_op jit(solution)/shard_map/ppermute | solution.py:20
  113.5 1.0 collective-permute-done.6
  115.1 3.3 %fusion.9 = bf16[1,16,16,192]{3,2,1,0:T(8,128)(2,1)} fusion(f32[1,22,22,192]{3,2,1,0:T(8,128)S(1)} %maximum_convert_fusion.1, f32[192]{0:T(256)S(1)} %bitcast.229, f32[192]{0:T(256)} %bitcast.47, f32[192]{0:T(256)S(1)} %bitcast.137, f32[192]{0:T(256)S(1)} %bitcast.139, f32[192]{0:T(256)S(1)} %bitcast.141, f32[192]{0:T(256)S(1)} %bitcast.143, ...), kind=kLoop, calls=%fused_computation.19 | loop fusion | flops 5013504 | bytes 9869056 | tf_op jit(solution)/shard_map/convert_element_type | solution.py:149
  118.4 86.5 %all-reduce.4.cloned.1.call-done = (f32[192,768]{1,0:T(8,128)}, f32[768,192]{0,1:T(8,128)}) async-done(((f32[192,768]{1,0:T(8,128)}, f32[768,192]{0,1:T(8,128)}), (f32[192,768]{1,0:T(8,128)}, f32[768,192]{0,1:T(8,128)})) %all-reduce.4.cloned.1.call-update) | async-done | bytes 1179664 | tf_op jit(solution)/shard_map/psum | solution.py:159
  204.8 2.0 broadcast_multiply_fusion
  206.8 0.9 broadcast_multiply_fusion.1
  (234 shorter events, 6.7 us)
Async XLA Ops:
  7.2 23.2 %copy-start = (bf16[768,192]{0,1:T(8,128)(2,1)S(1)}, bf16[768,192]{0,1:T(8,128)(2,1)}, u32[]{:S(2)}) copy-start(bf16[768,192]{0,1:T(8,128)(2,1)} %param.21) | copy-start | bytes 884740
  7.2 197.7 %all-reduce.4.cloned.1.call-start = ((), (), s32[]{:S(2)}) async-start(), calls=%async_computation | async-start | bytes 2359296 | tf_op jit(solution)/shard_map/psum | solution.py:159
  9.0 6.5 %collective-permute-start = (bf16[1,3,16,192]{3,2,1,0:T(8,128)(2,1)S(1)}, bf16[1,3,16,192]{3,2,1,0:T(8,128)(2,1)S(1)}, u32[]{:S(2)}, u32[]{:S(2)}) collective-permute-start(bf16[1,3,16,192]{3,2,1,0:T(8,128)(2,1)S(1)} %get-tuple-element.86), channel_id=1, source_target_pairs={{0,2},{1,3},{4,6},{5,7},{8,10},{9,11},{12,14},{13,15},{16,18},{17,... | collective-permute-start | bytes 55304 | tf_op jit(solution)/shard_map/ppermute | solution.py:17
  13.9 5.7 %collective-permute-start.1 = (bf16[1,3,16,192]{3,2,1,0:T(8,128)(2,1)S(1)}, bf16[1,3,16,192]{3,2,1,0:T(8,128)(2,1)S(1)}, u32[]{:S(2)}, u32[]{:S(2)}) collective-permute-start(bf16[1,3,16,192]{3,2,1,0:T(8,128)(2,1)S(1)} %get-tuple-element.87), channel_id=1, source_target_pairs={{2,0},{3,1},{6,4},{7,5},{10,8},{11,9},{14,12},{15,13},{18,16},{19,... | collective-permute-start | bytes 55304 | tf_op jit(solution)/shard_map/ppermute | solution.py:20
  15.3 10.7 %copy-start.8 = (f32[1,1,192]{2,1,0:T(1,128)}, f32[1,1,192]{2,1,0:T(1,128)S(1)}, u32[]{:S(2)}) copy-start(f32[1,1,192]{2,1,0:T(1,128)S(1)} %get-tuple-element.97) | copy-start | bytes 2308
  15.3 10.7 %copy-start.10 = (f32[1,1,192]{2,1,0:T(1,128)}, f32[1,1,192]{2,1,0:T(1,128)S(1)}, u32[]{:S(2)}) copy-start(f32[1,1,192]{2,1,0:T(1,128)S(1)} %get-tuple-element.98) | copy-start | bytes 2308
  15.3 10.7 %copy-start.12 = (f32[1,1,192]{2,1,0:T(1,128)}, f32[1,1,192]{2,1,0:T(1,128)S(1)}, u32[]{:S(2)}) copy-start(f32[1,1,192]{2,1,0:T(1,128)S(1)} %get-tuple-element.99) | copy-start | bytes 2308
  15.3 10.7 %copy-start.14 = (f32[1,1,192]{2,1,0:T(1,128)}, f32[1,1,192]{2,1,0:T(1,128)S(1)}, u32[]{:S(2)}) copy-start(f32[1,1,192]{2,1,0:T(1,128)S(1)} %get-tuple-element.100) | copy-start | bytes 2308
  15.3 10.7 %copy-start.16 = (f32[1,1,192]{2,1,0:T(1,128)}, f32[1,1,192]{2,1,0:T(1,128)S(1)}, u32[]{:S(2)}) copy-start(f32[1,1,192]{2,1,0:T(1,128)S(1)} %get-tuple-element.101) | copy-start | bytes 2308
  15.3 10.7 %copy-start.18 = (f32[1,1,192]{2,1,0:T(1,128)}, f32[1,1,192]{2,1,0:T(1,128)S(1)}, u32[]{:S(2)}) copy-start(f32[1,1,192]{2,1,0:T(1,128)S(1)} %get-tuple-element.102) | copy-start | bytes 2308
  15.3 10.7 %copy-start.20 = (f32[1,1,192]{2,1,0:T(1,128)}, f32[1,1,192]{2,1,0:T(1,128)S(1)}, u32[]{:S(2)}) copy-start(f32[1,1,192]{2,1,0:T(1,128)S(1)} %get-tuple-element.103) | copy-start | bytes 2308
  15.3 10.7 %copy-start.22 = (f32[1,1,192]{2,1,0:T(1,128)}, f32[1,1,192]{2,1,0:T(1,128)S(1)}, u32[]{:S(2)}) copy-start(f32[1,1,192]{2,1,0:T(1,128)S(1)} %get-tuple-element.104) | copy-start | bytes 2308
  15.3 10.7 %copy-start.24 = (f32[1,1,192]{2,1,0:T(1,128)}, f32[1,1,192]{2,1,0:T(1,128)S(1)}, u32[]{:S(2)}) copy-start(f32[1,1,192]{2,1,0:T(1,128)S(1)} %get-tuple-element.105) | copy-start | bytes 2308
  15.4 10.7 %copy-start.26 = (f32[1,1,192]{2,1,0:T(1,128)}, f32[1,1,192]{2,1,0:T(1,128)S(1)}, u32[]{:S(2)}) copy-start(f32[1,1,192]{2,1,0:T(1,128)S(1)} %get-tuple-element.106) | copy-start | bytes 2308
  15.4 10.7 %copy-start.28 = (f32[1,1,192]{2,1,0:T(1,128)}, f32[1,1,192]{2,1,0:T(1,128)S(1)}, u32[]{:S(2)}) copy-start(f32[1,1,192]{2,1,0:T(1,128)S(1)} %get-tuple-element.107) | copy-start | bytes 2308
  15.4 10.7 %copy-start.30 = (f32[1,1,192]{2,1,0:T(1,128)}, f32[1,1,192]{2,1,0:T(1,128)S(1)}, u32[]{:S(2)}) copy-start(f32[1,1,192]{2,1,0:T(1,128)S(1)} %get-tuple-element.108) | copy-start | bytes 2308
  15.4 10.7 %copy-start.32 = (f32[1,1,192]{2,1,0:T(1,128)}, f32[1,1,192]{2,1,0:T(1,128)S(1)}, u32[]{:S(2)}) copy-start(f32[1,1,192]{2,1,0:T(1,128)S(1)} %get-tuple-element.109) | copy-start | bytes 2308
  15.4 10.7 %copy-start.34 = (f32[1,1,192]{2,1,0:T(1,128)}, f32[1,1,192]{2,1,0:T(1,128)S(1)}, u32[]{:S(2)}) copy-start(f32[1,1,192]{2,1,0:T(1,128)S(1)} %get-tuple-element.110) | copy-start | bytes 2308
  15.4 10.7 %copy-start.36 = (f32[1,1,192]{2,1,0:T(1,128)}, f32[1,1,192]{2,1,0:T(1,128)S(1)}, u32[]{:S(2)}) copy-start(f32[1,1,192]{2,1,0:T(1,128)S(1)} %get-tuple-element.111) | copy-start | bytes 2308
  15.4 10.7 %copy-start.38 = (f32[1,1,192]{2,1,0:T(1,128)}, f32[1,1,192]{2,1,0:T(1,128)S(1)}, u32[]{:S(2)}) copy-start(f32[1,1,192]{2,1,0:T(1,128)S(1)} %get-tuple-element.112) | copy-start | bytes 2308
  15.5 10.7 %copy-start.40 = (f32[1,1,192]{2,1,0:T(1,128)}, f32[1,1,192]{2,1,0:T(1,128)S(1)}, u32[]{:S(2)}) copy-start(f32[1,1,192]{2,1,0:T(1,128)S(1)} %get-tuple-element.113) | copy-start | bytes 2308
  15.5 10.7 %copy-start.42 = (f32[1,1,192]{2,1,0:T(1,128)}, f32[1,1,192]{2,1,0:T(1,128)S(1)}, u32[]{:S(2)}) copy-start(f32[1,1,192]{2,1,0:T(1,128)S(1)} %get-tuple-element.114) | copy-start | bytes 2308
  15.5 10.7 %copy-start.44 = (f32[1,1,192]{2,1,0:T(1,128)}, f32[1,1,192]{2,1,0:T(1,128)S(1)}, u32[]{:S(2)}) copy-start(f32[1,1,192]{2,1,0:T(1,128)S(1)} %get-tuple-element.115) | copy-start | bytes 2308
  15.5 10.7 %copy-start.46 = (f32[1,1,192]{2,1,0:T(1,128)}, f32[1,1,192]{2,1,0:T(1,128)S(1)}, u32[]{:S(2)}) copy-start(f32[1,1,192]{2,1,0:T(1,128)S(1)} %get-tuple-element.116) | copy-start | bytes 2308
  15.5 10.7 %copy-start.48 = (f32[1,1,192]{2,1,0:T(1,128)}, f32[1,1,192]{2,1,0:T(1,128)S(1)}, u32[]{:S(2)}) copy-start(f32[1,1,192]{2,1,0:T(1,128)S(1)} %get-tuple-element.117) | copy-start | bytes 2308
  15.5 10.7 %copy-start.50 = (f32[1,1,192]{2,1,0:T(1,128)}, f32[1,1,192]{2,1,0:T(1,128)S(1)}, u32[]{:S(2)}) copy-start(f32[1,1,192]{2,1,0:T(1,128)S(1)} %get-tuple-element.118) | copy-start | bytes 2308
  19.7 6.0 %collective-permute-start.2 = (bf16[1,22,3,192]{3,2,1,0:T(4,128)(2,1)S(1)}, bf16[1,22,3,192]{3,2,1,0:T(4,128)(2,1)S(1)}, u32[]{:S(2)}, u32[]{:S(2)}) collective-permute-start(bf16[1,22,3,192]{3,2,1,0:T(4,128)(2,1)S(1)} %get-tuple-element.80), channel_id=1, source_target_pairs={{0,4},{4,8},{8,12},{12,0},{1,5},{5,9},{9,13},{13,1},{2,6},{6,10},{... | collective-permute-start | bytes 76040 | tf_op jit(solution)/shard_map/ppermute | solution.py:17
  21.3 4.5 %collective-permute-start.3 = (bf16[1,22,3,192]{3,2,1,0:T(4,128)(2,1)S(1)}, bf16[1,22,3,192]{3,2,1,0:T(4,128)(2,1)S(1)}, u32[]{:S(2)}, u32[]{:S(2)}) collective-permute-start(bf16[1,22,3,192]{3,2,1,0:T(4,128)(2,1)S(1)} %get-tuple-element.81), channel_id=1, source_target_pairs={{4,0},{8,4},{12,8},{0,12},{5,1},{9,5},{13,9},{1,13},{6,2},{10,6},{... | collective-permute-start | bytes 76040 | tf_op jit(solution)/shard_map/ppermute | solution.py:20
  101.6 3.7 %collective-permute-start.4 = (bf16[1,3,16,192]{3,2,1,0:T(8,128)(2,1)S(1)}, bf16[1,3,16,192]{3,2,1,0:T(8,128)(2,1)S(1)}, u32[]{:S(2)}, u32[]{:S(2)}) collective-permute-start(bf16[1,3,16,192]{3,2,1,0:T(8,128)(2,1)S(1)} %get-tuple-element.84), channel_id=1, source_target_pairs={{0,2},{1,3},{4,6},{5,7},{8,10},{9,11},{12,14},{13,15},{16,18},{17,... | collective-permute-start | bytes 55304 | tf_op jit(solution)/shard_map/ppermute | solution.py:17
  102.9 5.7 %collective-permute-start.5 = (bf16[1,3,16,192]{3,2,1,0:T(8,128)(2,1)S(1)}, bf16[1,3,16,192]{3,2,1,0:T(8,128)(2,1)S(1)}, u32[]{:S(2)}, u32[]{:S(2)}) collective-permute-start(bf16[1,3,16,192]{3,2,1,0:T(8,128)(2,1)S(1)} %get-tuple-element.85), channel_id=1, source_target_pairs={{2,0},{3,1},{6,4},{7,5},{10,8},{11,9},{14,12},{15,13},{18,16},{19,... | collective-permute-start | bytes 55304 | tf_op jit(solution)/shard_map/ppermute | solution.py:20
  108.7 5.9 %collective-permute-start.6 = (bf16[1,22,3,192]{3,2,1,0:T(4,128)(2,1)S(1)}, bf16[1,22,3,192]{3,2,1,0:T(4,128)(2,1)S(1)}, u32[]{:S(2)}, u32[]{:S(2)}) collective-permute-start(bf16[1,22,3,192]{3,2,1,0:T(4,128)(2,1)S(1)} %get-tuple-element.78), channel_id=1, source_target_pairs={{0,4},{4,8},{8,12},{12,0},{1,5},{5,9},{9,13},{13,1},{2,6},{6,10},{... | collective-permute-start | bytes 76040 | tf_op jit(solution)/shard_map/ppermute | solution.py:17
  108.7 5.8 %collective-permute-start.7 = (bf16[1,22,3,192]{3,2,1,0:T(4,128)(2,1)S(1)}, bf16[1,22,3,192]{3,2,1,0:T(4,128)(2,1)S(1)}, u32[]{:S(2)}, u32[]{:S(2)}) collective-permute-start(bf16[1,22,3,192]{3,2,1,0:T(4,128)(2,1)S(1)} %get-tuple-element.79), channel_id=1, source_target_pairs={{4,0},{8,4},{12,8},{0,12},{5,1},{9,5},{13,9},{1,13},{6,2},{10,6},{... | collective-permute-start | bytes 76040 | tf_op jit(solution)/shard_map/ppermute | solution.py:20
  (72 other events, 180.3 us)
Sparse Core Ops, SparseCore 0:
  113.2 91.5 all-reduce.3
where the time goes:
time: 215 us
  waiting for transfers between devices  96.5 us (45%)
  blocking collectives  58.4 us (27%)
  other arithmetic  17.3 us (8%)
  starting transfers between devices  16.5 us (8%)
  between operations  15.6 us (7%)
  matrix products  5.21 us (2%)
  local copies, waits for them, and re-layouts  5 us (2%)
    psum x1, waiting for transfers between devices, body(): lax.psum((local[0], local[1], local[2], local[3], local[4], local[5], loc...  86.5 us
    psum x1, blocking collectives, body(): lax.psum((local[0], local[1], local[2], local[3], local[4], local[5], loc...  58.4 us
    ppermute x4, starting transfers between devices, padded_2(): lax.ppermute(lax.slice_in_dim(block, 0, width, axis=dim), axis, backward)  8.64 us
    ppermute x4, starting transfers between devices, padded_2(): lax.ppermute(lax.slice_in_dim(block, block.shape[dim] - width, None, axis...  7.84 us
    ppermute x4, waiting for transfers between devices, padded_2(): lax.ppermute(lax.slice_in_dim(block, 0, width, axis=dim), axis, backward)  7.5 us
    mul x7, other arithmetic, body(): finals = [piece * factor for piece in summed]  5.76 us
  transfers between devices with their start and end apart: 9, of which 6 were waited for; matrix products, arithmetic and copies ran while one was open for 3% of the time, Pallas kernels for 0%

commit v1 on v0

--- a/solution.py
+++ b/solution.py
@@ -3,6 +3,7 @@
 import jax.numpy as jnp
 from jax import lax
 from jax.sharding import PartitionSpec as P
+from jax.lax import psum
 
 EPS = 1e-06
 
@@ -156,10 +157,19 @@
     ) + mlp_sums
     members = lax.axis_size("lon") * lax.axis_size("lat") * lax.axis_size("dp")
     factor = 1.0 / math.sqrt(snapshots * cells * members)
-    summed = lax.psum(
-        (local[0], local[1], local[2], local[3], local[4], local[5], local[6], local[7], local[8]),
-        ("lon", "lat", "dp"),
-    )
+    summed = (
+        local[0],
+        local[1],
+        local[2],
+        local[3],
+        local[4],
+        local[5],
+        local[6],
+        local[7],
+        local[8],
+    )
+    for pp in ("lon", ("lat", "dp")):
+        summed = psum(summed, axis_name=pp)
     finals = [piece * factor for piece in summed]
     return (
         block_out,

time: 215 us -> 156 us (0.73)
  waiting for transfers between devices: 96.5 us -> 60.7 us
  blocking collectives: 58.4 us -> 34.4 us
    psum x1 -> x2, waiting for transfers between devices: 86.5 us -> 51.9 us  [body(): summed = psum(summed, axis_name=pp)]
    psum x1 -> x2, blocking collectives: 58.4 us -> 34.4 us  [body(): summed = psum(summed, axis_name=pp)]
    ppermute x4, waiting for transfers between devices: 7.5 us -> 4.5 us  [padded_2(): lax.ppermute(lax.slice_in_dim(block, 0, width, axis=dim), axis, backward)]
  transfers between devices with their start and end apart: 9 -> 10, of which waited for: 6 -> 7; matrix products, arithmetic and copies ran while one was open for 3% -> 5% of each run, Pallas kernels for 0% -> 0%
where the time goes in v1:
time: 156 us; the launch traced here: 155 us
  waiting for transfers between devices  60.7 us (39%)
  blocking collectives  34.4 us (22%)
  other arithmetic  17.2 us (11%)
  starting transfers between devices  16.9 us (11%)
  between operations  15.6 us (10%)
  local copies, waits for them, and re-layouts  5.45 us (3%)
  matrix products  5.21 us (3%)
    psum x2, waiting for transfers between devices, body(): summed = psum(summed, axis_name=pp)  51.9 us
    psum x2, blocking collectives, body(): summed = psum(summed, axis_name=pp)  34.4 us
    ppermute x4, starting transfers between devices, padded_2(): lax.ppermute(lax.slice_in_dim(block, 0, width, axis=dim), axis, backward)  8.64 us
    ppermute x4, starting transfers between devices, padded_2(): lax.ppermute(lax.slice_in_dim(block, block.shape[dim] - width, None, axis...  8.19 us
    mul x7, other arithmetic, body(): finals = [piece * factor for piece in summed]  5.76 us
    ppermute x4, waiting for transfers between devices, padded_2(): lax.ppermute(lax.slice_in_dim(block, 0, width, axis=dim), axis, backward)  4.5 us
    unnamed x196, local copies, waits for them, and re-layouts  4.23 us
    ppermute x4, waiting for transfers between devices, padded_2(): lax.ppermute(lax.slice_in_dim(block, block.shape[dim] - width, None, axis...  4.22 us
  transfers between devices with their start and end apart: 10, of which 7 were waited for; matrix products, arithmetic and copies ran while one was open for 5% of the time, Pallas kernels for 0%

profile of v1, /device:TPU:0, one launch (start us, length us, event | category | flops | bytes accessed | tf_op | source)
XLA Modules:
  0.0 155.3 jit_solution(12752770792426406468)
XLA Ops:
  7.2 0.8 fusion.69
  8.0 1.0 broadcast_multiply_fusion.2
  9.0 4.9 %collective-permute-start = (bf16[1,3,16,192]{3,2,1,0:T(8,128)(2,1)S(1)}, bf16[1,3,16,192]{3,2,1,0:T(8,128)(2,1)S(1)}, u32[]{:S(2)}, u32[]{:S(2)}) collective-permute-start(bf16[1,3,16,192]{3,2,1,0:T(8,128)(2,1)S(1)} %get-tuple-element.95), channel_id=1, source_target_pairs={{0,2},{1,3},{4,6},{5,7},{8,10},{9,11},{12,14},{13,15},{16,18},{17,... | collective-permute-start | bytes 55304 | tf_op jit(solution)/shard_map/ppermute | solution.py:18
  13.9 1.3 collective-permute-start.1
  15.6 4.1 %collective-permute-done.1 = bf16[1,3,16,192]{3,2,1,0:T(8,128)(2,1)S(1)} collective-permute-done((bf16[1,3,16,192]{3,2,1,0:T(8,128)(2,1)S(1)}, bf16[1,3,16,192]{3,2,1,0:T(8,128)(2,1)S(1)}, u32[]{:S(2)}, u32[]{:S(2)}) %collective-permute-start.1) | collective-permute-done | bytes 18464 | tf_op jit(solution)/shard_map/ppermute | solution.py:21
  19.7 1.6 %collective-permute-start.2 = (bf16[1,22,3,192]{3,2,1,0:T(4,128)(2,1)S(1)}, bf16[1,22,3,192]{3,2,1,0:T(4,128)(2,1)S(1)}, u32[]{:S(2)}, u32[]{:S(2)}) collective-permute-start(bf16[1,22,3,192]{3,2,1,0:T(4,128)(2,1)S(1)} %get-tuple-element.89), channel_id=1, source_target_pairs={{0,4},{4,8},{8,12},{12,0},{1,5},{5,9},{9,13},{13,1},{2,6},{6,10},{... | collective-permute-start | bytes 76040 | tf_op jit(solution)/shard_map/ppermute | solution.py:18
  21.3 2.2 %collective-permute-start.3 = (bf16[1,22,3,192]{3,2,1,0:T(4,128)(2,1)S(1)}, bf16[1,22,3,192]{3,2,1,0:T(4,128)(2,1)S(1)}, u32[]{:S(2)}, u32[]{:S(2)}) collective-permute-start(bf16[1,22,3,192]{3,2,1,0:T(4,128)(2,1)S(1)} %get-tuple-element.90), channel_id=1, source_target_pairs={{4,0},{8,4},{12,8},{0,12},{5,1},{9,5},{13,9},{1,13},{6,2},{10,6},{... | collective-permute-start | bytes 76040 | tf_op jit(solution)/shard_map/ppermute | solution.py:21
  24.2 1.5 collective-permute-done.2
  26.7 2.4 %fusion.63 = (f32[16,16]{1,0:T(8,128)S(1)}, f32[1,16,16,192]{3,2,1,0:T(8,128)S(1)}) fusion(f32[192]{0:T(256)S(1)} %copy-done.90, f32[192]{0:T(256)S(1)} %bitcast.228, f32[1,22,22,192]{3,2,1,0:T(8,128)S(1)} %maximum_convert_fusion, f32[192]{0:T(256)} %bitcast.47, f32[192]{0:T(256)S(1)} %bitcast.136, f32[192]{0:T(256)S(1)} %bitcast.138, f32[192]{0:T(256)S(1)} %bitcast.140, ...), kind=kLoop, calls=%fused_computation.208 | loop fusion | flops 4865792 | bytes 9869824 | tf_op jit(solution)/shard_map/reduce_sum | solution.py:118
  29.4 0.6 copy-done.1
  31.3 0.7 copy-done.3
  32.1 1.4 multiply_reduce_fusion
  33.5 1.3 fusion.70
  34.7 1.0 fusion.62
  36.2 0.7 multiply_reduce_fusion.2
  38.5 1.2 fusion.61
  39.8 1.1 fusion.57
  41.0 1.6 %collective-permute-start.4 = (bf16[1,3,16,192]{3,2,1,0:T(8,128)(2,1)S(1)}, bf16[1,3,16,192]{3,2,1,0:T(8,128)(2,1)S(1)}, u32[]{:S(2)}, u32[]{:S(2)}) collective-permute-start(bf16[1,3,16,192]{3,2,1,0:T(8,128)(2,1)S(1)} %get-tuple-element.93), channel_id=1, source_target_pairs={{0,2},{1,3},{4,6},{5,7},{8,10},{9,11},{12,14},{13,15},{16,18},{17,... | collective-permute-start | bytes 55304 | tf_op jit(solution)/shard_map/ppermute | solution.py:18
  42.6 1.3 collective-permute-start.5
  44.3 0.6 copy-done.89
  44.9 22.0 %all-reduce.2 = (f32[7,7,192]{2,1,0:T(8,128)S(1)}, f32[192]{0:T(256)S(1)}, f32[192]{0:T(256)S(1)}, f32[192]{0:T(256)S(1)}, f32[768]{0:T(1024)S(1)}, /*index=5*/f32[192]{0:T(256)S(1)}, f32[192]{0:T(256)S(1)}) all-reduce(f32[7,7,192]{2,1,0:T(8,128)S(1)} %constant_dynamic-update-slice_fusi, ...), channel_id=1, replica_groups=mesh['groups'=2,'lon'=4,'lat'=2,'dp'=2] {'lon'}, use_global_device_ids=true, to_apply=%region_53.0 | all-reduce | flops 11136 | bytes 89088 | tf_op jit(solution)/shard_map/psum | solution.py:172
  67.0 12.3 %all-reduce = (f32[7,7,192]{2,1,0:T(8,128)S(1)}, f32[192]{0:T(256)S(1)}, f32[192]{0:T(256)S(1)}, f32[192]{0:T(256)S(1)}, f32[768]{0:T(1024)S(1)}, /*index=5*/f32[192]{0:T(256)S(1)}, f32[192]{0:T(256)S(1)}) all-reduce(f32[7,7,192]{2,1,0:T(8,128)S(1)} %get-tuple-element.74, ...), channel_id=1, replica_groups=mesh['groups'=2,'lon'=4,'lat'=2,'dp'=2] {'lat','dp'}, use_global_device_ids=true, to_apply=%region_54.0 | all-reduce | flops 11136 | bytes 89088 | tf_op jit(solution)/shard_map/psum | solution.py:172
  79.3 0.6 broadcast_multiply_fusion.7
  79.9 0.6 broadcast_multiply_fusion.6
  80.5 0.6 broadcast_multiply_fusion.3
  81.8 3.8 %collective-permute-start.7 = (bf16[1,22,3,192]{3,2,1,0:T(4,128)(2,1)S(1)}, bf16[1,22,3,192]{3,2,1,0:T(4,128)(2,1)S(1)}, u32[]{:S(2)}, u32[]{:S(2)}) collective-permute-start(bf16[1,22,3,192]{3,2,1,0:T(4,128)(2,1)S(1)} %get-tuple-element.88), channel_id=1, source_target_pairs={{4,0},{8,4},{12,8},{0,12},{5,1},{9,5},{13,9},{1,13},{6,2},{10,6},{... | collective-permute-start | bytes 76040 | tf_op jit(solution)/shard_map/ppermute | solution.py:21
  86.2 2.7 %collective-permute-done.6 = bf16[1,22,3,192]{3,2,1,0:T(4,128)(2,1)S(1)} collective-permute-done((bf16[1,22,3,192]{3,2,1,0:T(4,128)(2,1)S(1)}, bf16[1,22,3,192]{3,2,1,0:T(4,128)(2,1)S(1)}, u32[]{:S(2)}, u32[]{:S(2)}) %collective-permute-start.6) | collective-permute-done | bytes 25376 | tf_op jit(solution)/shard_map/ppermute | solution.py:18
  89.3 16.8 %all-reduce.9.cloned.1.call-done = (f32[192,768]{1,0:T(8,128)}, f32[768,192]{0,1:T(8,128)}) async-done(((f32[192,768]{1,0:T(8,128)}, f32[768,192]{0,1:T(8,128)}), (f32[192,768]{1,0:T(8,128)}, f32[768,192]{0,1:T(8,128)})) %all-reduce.9.cloned.1.call-update) | async-done | bytes 1179664 | tf_op jit(solution)/shard_map/psum | solution.py:172
  107.3 3.2 %fusion.9 = bf16[1,16,16,192]{3,2,1,0:T(8,128)(2,1)} fusion(f32[1,22,22,192]{3,2,1,0:T(8,128)S(1)} %maximum_convert_fusion.1, f32[192]{0:T(256)S(1)} %bitcast.229, f32[192]{0:T(256)} %bitcast.47, f32[192]{0:T(256)S(1)} %bitcast.137, f32[192]{0:T(256)S(1)} %bitcast.139, f32[192]{0:T(256)S(1)} %bitcast.141, f32[192]{0:T(256)S(1)} %bitcast.143, ...), kind=kLoop, calls=%fused_computation.19 | loop fusion | flops 5013504 | bytes 9869056 | tf_op jit(solution)/shard_map/convert_element_type | solution.py:150
  110.5 35.2 %all-reduce.7.cloned.1.call-done = (f32[192,768]{1,0:T(8,128)}, f32[768,192]{0,1:T(8,128)}) async-done(((f32[192,768]{1,0:T(8,128)}, f32[768,192]{0,1:T(8,128)}), (f32[192,768]{1,0:T(8,128)}, f32[768,192]{0,1:T(8,128)})) %all-reduce.7.cloned.1.call-update) | async-done | bytes 1179664 | tf_op jit(solution)/shard_map/psum | solution.py:172
  145.7 2.0 %broadcast_multiply_fusion = f32[768,192]{0,1:T(8,128)} fusion(f32[768,192]{0,1:T(8,128)} %get-tuple-element.73), kind=kLoop, calls=%fused_computation.11 | loop fusion | flops 147456 | bytes 1179648 | tf_op jit(solution)/shard_map/mul | solution.py:173
  147.6 0.9 broadcast_multiply_fusion.1
  (238 shorter events, 8.0 us)
Async XLA Ops:
  7.2 23.1 %copy-start = (bf16[768,192]{0,1:T(8,128)(2,1)S(1)}, bf16[768,192]{0,1:T(8,128)(2,1)}, u32[]{:S(2)}) copy-start(bf16[768,192]{0,1:T(8,128)(2,1)} %param.21) | copy-start | bytes 884740
  7.2 98.8 %all-reduce.9.cloned.1.call-start = ((), (), s32[]{:S(2)}) async-start(), calls=%async_computation.1 | async-start | bytes 2359296 | tf_op jit(solution)/shard_map/psum | solution.py:172
  9.0 6.5 %collective-permute-start = (bf16[1,3,16,192]{3,2,1,0:T(8,128)(2,1)S(1)}, bf16[1,3,16,192]{3,2,1,0:T(8,128)(2,1)S(1)}, u32[]{:S(2)}, u32[]{:S(2)}) collective-permute-start(bf16[1,3,16,192]{3,2,1,0:T(8,128)(2,1)S(1)} %get-tuple-element.95), channel_id=1, source_target_pairs={{0,2},{1,3},{4,6},{5,7},{8,10},{9,11},{12,14},{13,15},{16,18},{17,... | collective-permute-start | bytes 55304 | tf_op jit(solution)/shard_map/ppermute | solution.py:18
  13.9 5.7 %collective-permute-start.1 = (bf16[1,3,16,192]{3,2,1,0:T(8,128)(2,1)S(1)}, bf16[1,3,16,192]{3,2,1,0:T(8,128)(2,1)S(1)}, u32[]{:S(2)}, u32[]{:S(2)}) collective-permute-start(bf16[1,3,16,192]{3,2,1,0:T(8,128)(2,1)S(1)} %get-tuple-element.96), channel_id=1, source_target_pairs={{2,0},{3,1},{6,4},{7,5},{10,8},{11,9},{14,12},{15,13},{18,16},{19,... | collective-permute-start | bytes 55304 | tf_op jit(solution)/shard_map/ppermute | solution.py:21
  15.3 10.7 %copy-start.8 = (f32[1,1,192]{2,1,0:T(1,128)}, f32[1,1,192]{2,1,0:T(1,128)S(1)}, u32[]{:S(2)}) copy-start(f32[1,1,192]{2,1,0:T(1,128)S(1)} %get-tuple-element.106) | copy-start | bytes 2308
  15.3 10.7 %copy-start.10 = (f32[1,1,192]{2,1,0:T(1,128)}, f32[1,1,192]{2,1,0:T(1,128)S(1)}, u32[]{:S(2)}) copy-start(f32[1,1,192]{2,1,0:T(1,128)S(1)} %get-tuple-element.107) | copy-start | bytes 2308
  15.3 10.7 %copy-start.12 = (f32[1,1,192]{2,1,0:T(1,128)}, f32[1,1,192]{2,1,0:T(1,128)S(1)}, u32[]{:S(2)}) copy-start(f32[1,1,192]{2,1,0:T(1,128)S(1)} %get-tuple-element.108) | copy-start | bytes 2308
  15.3 10.7 %copy-start.14 = (f32[1,1,192]{2,1,0:T(1,128)}, f32[1,1,192]{2,1,0:T(1,128)S(1)}, u32[]{:S(2)}) copy-start(f32[1,1,192]{2,1,0:T(1,128)S(1)} %get-tuple-element.109) | copy-start | bytes 2308
  15.3 10.7 %copy-start.16 = (f32[1,1,192]{2,1,0:T(1,128)}, f32[1,1,192]{2,1,0:T(1,128)S(1)}, u32[]{:S(2)}) copy-start(f32[1,1,192]{2,1,0:T(1,128)S(1)} %get-tuple-element.110) | copy-start | bytes 2308
  15.3 10.7 %copy-start.18 = (f32[1,1,192]{2,1,0:T(1,128)}, f32[1,1,192]{2,1,0:T(1,128)S(1)}, u32[]{:S(2)}) copy-start(f32[1,1,192]{2,1,0:T(1,128)S(1)} %get-tuple-element.111) | copy-start | bytes 2308
  15.3 10.7 %copy-start.20 = (f32[1,1,192]{2,1,0:T(1,128)}, f32[1,1,192]{2,1,0:T(1,128)S(1)}, u32[]{:S(2)}) copy-start(f32[1,1,192]{2,1,0:T(1,128)S(1)} %get-tuple-element.112) | copy-start | bytes 2308
  15.3 10.7 %copy-start.22 = (f32[1,1,192]{2,1,0:T(1,128)}, f32[1,1,192]{2,1,0:T(1,128)S(1)}, u32[]{:S(2)}) copy-start(f32[1,1,192]{2,1,0:T(1,128)S(1)} %get-tuple-element.113) | copy-start | bytes 2308
  15.3 10.7 %copy-start.24 = (f32[1,1,192]{2,1,0:T(1,128)}, f32[1,1,192]{2,1,0:T(1,128)S(1)}, u32[]{:S(2)}) copy-start(f32[1,1,192]{2,1,0:T(1,128)S(1)} %get-tuple-element.114) | copy-start | bytes 2308
  15.4 10.7 %copy-start.26 = (f32[1,1,192]{2,1,0:T(1,128)}, f32[1,1,192]{2,1,0:T(1,128)S(1)}, u32[]{:S(2)}) copy-start(f32[1,1,192]{2,1,0:T(1,128)S(1)} %get-tuple-element.115) | copy-start | bytes 2308
  15.4 10.7 %copy-start.28 = (f32[1,1,192]{2,1,0:T(1,128)}, f32[1,1,192]{2,1,0:T(1,128)S(1)}, u32[]{:S(2)}) copy-start(f32[1,1,192]{2,1,0:T(1,128)S(1)} %get-tuple-element.116) | copy-start | bytes 2308
  15.4 10.7 %copy-start.30 = (f32[1,1,192]{2,1,0:T(1,128)}, f32[1,1,192]{2,1,0:T(1,128)S(1)}, u32[]{:S(2)}) copy-start(f32[1,1,192]{2,1,0:T(1,128)S(1)} %get-tuple-element.117) | copy-start | bytes 2308
  15.4 10.7 %copy-start.32 = (f32[1,1,192]{2,1,0:T(1,128)}, f32[1,1,192]{2,1,0:T(1,128)S(1)}, u32[]{:S(2)}) copy-start(f32[1,1,192]{2,1,0:T(1,128)S(1)} %get-tuple-element.118) | copy-start | bytes 2308
  15.4 10.7 %copy-start.34 = (f32[1,1,192]{2,1,0:T(1,128)}, f32[1,1,192]{2,1,0:T(1,128)S(1)}, u32[]{:S(2)}) copy-start(f32[1,1,192]{2,1,0:T(1,128)S(1)} %get-tuple-element.119) | copy-start | bytes 2308
  15.4 10.7 %copy-start.36 = (f32[1,1,192]{2,1,0:T(1,128)}, f32[1,1,192]{2,1,0:T(1,128)S(1)}, u32[]{:S(2)}) copy-start(f32[1,1,192]{2,1,0:T(1,128)S(1)} %get-tuple-element.120) | copy-start | bytes 2308
  15.4 10.7 %copy-start.38 = (f32[1,1,192]{2,1,0:T(1,128)}, f32[1,1,192]{2,1,0:T(1,128)S(1)}, u32[]{:S(2)}) copy-start(f32[1,1,192]{2,1,0:T(1,128)S(1)} %get-tuple-element.121) | copy-start | bytes 2308
  15.5 10.7 %copy-start.40 = (f32[1,1,192]{2,1,0:T(1,128)}, f32[1,1,192]{2,1,0:T(1,128)S(1)}, u32[]{:S(2)}) copy-start(f32[1,1,192]{2,1,0:T(1,128)S(1)} %get-tuple-element.122) | copy-start | bytes 2308
  15.5 10.7 %copy-start.42 = (f32[1,1,192]{2,1,0:T(1,128)}, f32[1,1,192]{2,1,0:T(1,128)S(1)}, u32[]{:S(2)}) copy-start(f32[1,1,192]{2,1,0:T(1,128)S(1)} %get-tuple-element.123) | copy-start | bytes 2308
  15.5 10.7 %copy-start.44 = (f32[1,1,192]{2,1,0:T(1,128)}, f32[1,1,192]{2,1,0:T(1,128)S(1)}, u32[]{:S(2)}) copy-start(f32[1,1,192]{2,1,0:T(1,128)S(1)} %get-tuple-element.124) | copy-start | bytes 2308
  15.5 10.7 %copy-start.46 = (f32[1,1,192]{2,1,0:T(1,128)}, f32[1,1,192]{2,1,0:T(1,128)S(1)}, u32[]{:S(2)}) copy-start(f32[1,1,192]{2,1,0:T(1,128)S(1)} %get-tuple-element.125) | copy-start | bytes 2308
  15.5 10.7 %copy-start.48 = (f32[1,1,192]{2,1,0:T(1,128)}, f32[1,1,192]{2,1,0:T(1,128)S(1)}, u32[]{:S(2)}) copy-start(f32[1,1,192]{2,1,0:T(1,128)S(1)} %get-tuple-element.126) | copy-start | bytes 2308
  19.7 6.0 %collective-permute-start.2 = (bf16[1,22,3,192]{3,2,1,0:T(4,128)(2,1)S(1)}, bf16[1,22,3,192]{3,2,1,0:T(4,128)(2,1)S(1)}, u32[]{:S(2)}, u32[]{:S(2)}) collective-permute-start(bf16[1,22,3,192]{3,2,1,0:T(4,128)(2,1)S(1)} %get-tuple-element.89), channel_id=1, source_target_pairs={{0,4},{4,8},{8,12},{12,0},{1,5},{5,9},{9,13},{13,1},{2,6},{6,10},{... | collective-permute-start | bytes 76040 | tf_op jit(solution)/shard_map/ppermute | solution.py:18
  21.3 4.5 %collective-permute-start.3 = (bf16[1,22,3,192]{3,2,1,0:T(4,128)(2,1)S(1)}, bf16[1,22,3,192]{3,2,1,0:T(4,128)(2,1)S(1)}, u32[]{:S(2)}, u32[]{:S(2)}) collective-permute-start(bf16[1,22,3,192]{3,2,1,0:T(4,128)(2,1)S(1)} %get-tuple-element.90), channel_id=1, source_target_pairs={{4,0},{8,4},{12,8},{0,12},{5,1},{9,5},{13,9},{1,13},{6,2},{10,6},{... | collective-permute-start | bytes 76040 | tf_op jit(solution)/shard_map/ppermute | solution.py:21
  41.0 40.7 %collective-permute-start.4 = (bf16[1,3,16,192]{3,2,1,0:T(8,128)(2,1)S(1)}, bf16[1,3,16,192]{3,2,1,0:T(8,128)(2,1)S(1)}, u32[]{:S(2)}, u32[]{:S(2)}) collective-permute-start(bf16[1,3,16,192]{3,2,1,0:T(8,128)(2,1)S(1)} %get-tuple-element.93), channel_id=1, source_target_pairs={{0,2},{1,3},{4,6},{5,7},{8,10},{9,11},{12,14},{13,15},{16,18},{17,... | collective-permute-start | bytes 55304 | tf_op jit(solution)/shard_map/ppermute | solution.py:18
  42.6 39.1 %collective-permute-start.5 = (bf16[1,3,16,192]{3,2,1,0:T(8,128)(2,1)S(1)}, bf16[1,3,16,192]{3,2,1,0:T(8,128)(2,1)S(1)}, u32[]{:S(2)}, u32[]{:S(2)}) collective-permute-start(bf16[1,3,16,192]{3,2,1,0:T(8,128)(2,1)S(1)} %get-tuple-element.94), channel_id=1, source_target_pairs={{2,0},{3,1},{6,4},{7,5},{10,8},{11,9},{14,12},{15,13},{18,16},{19,... | collective-permute-start | bytes 55304 | tf_op jit(solution)/shard_map/ppermute | solution.py:21
  44.2 101.5 %all-reduce.7.cloned.1.call-start = ((), (), s32[]{:S(2)}) async-start(), calls=%async_computation | async-start | bytes 2359296 | tf_op jit(solution)/shard_map/psum | solution.py:172
  81.7 7.1 %collective-permute-start.6 = (bf16[1,22,3,192]{3,2,1,0:T(4,128)(2,1)S(1)}, bf16[1,22,3,192]{3,2,1,0:T(4,128)(2,1)S(1)}, u32[]{:S(2)}, u32[]{:S(2)}) collective-permute-start(bf16[1,22,3,192]{3,2,1,0:T(4,128)(2,1)S(1)} %get-tuple-element.87), channel_id=1, source_target_pairs={{0,4},{4,8},{8,12},{12,0},{1,5},{5,9},{9,13},{13,1},{2,6},{6,10},{... | collective-permute-start | bytes 76040 | tf_op jit(solution)/shard_map/ppermute | solution.py:18
  81.8 7.3 %collective-permute-start.7 = (bf16[1,22,3,192]{3,2,1,0:T(4,128)(2,1)S(1)}, bf16[1,22,3,192]{3,2,1,0:T(4,128)(2,1)S(1)}, u32[]{:S(2)}, u32[]{:S(2)}) collective-permute-start(bf16[1,22,3,192]{3,2,1,0:T(4,128)(2,1)S(1)} %get-tuple-element.88), channel_id=1, source_target_pairs={{4,0},{8,4},{12,8},{0,12},{5,1},{9,5},{13,9},{1,13},{6,2},{10,6},{... | collective-permute-start | bytes 76040 | tf_op jit(solution)/shard_map/ppermute | solution.py:21
  (73 other events, 165.7 us)
Sparse Core Ops, SparseCore 0:
  44.3 61.6 all-reduce.8
  108.4 37.2 all-reduce.6
